TPU v7x, 256 devices: a whole 4x4x8 slice. The times are simulated.
256 devices in a mesh: dp: 16 (over z_lo, x), tensor: 16 (over y, z_hi, core).
Axes of the slice: x: 4, y: 4, z: 8 (z_hi: 2, z_lo: 4; z = z_hi * 4 + z_lo), core: 2. Of those that a mesh axis runs over, the one named last changes fastest.
Arguments:
- out_grad: bfloat16 [2048, 5120], P('dp'), may hold values from -6 to 6
- gate_act: bfloat16 [2048, 25600], P('dp', 'tensor'), may hold values from -6 to 6
- up_act: bfloat16 [2048, 25600], P('dp', 'tensor'), may hold values from -6 to 6
- codes: int32 [5120, 25600], P('dp', 'tensor'), may hold values from 0 to 15
- zero_points: int32 [5120, 400], P('dp', 'tensor'), may hold values from 0 to 15
- scales: float32 [5120, 400], P('dp', 'tensor'), may hold values from 0.0009782797 to 0.003913119
- rotation: bfloat16 [1600, 1600], replicated, may hold values from -0.15625 to 0.15625
Outputs:
- grad_gate: bfloat16 [2048, 25600], P('dp', 'tensor')
- grad_up: bfloat16 [2048, 25600], P('dp', 'tensor')
- log_scale_grad: float32 [5120, 400], P('dp', 'tensor')
All inputs are finite; a program needn't handle non-finite values.
Results may differ from a plain program's by a relative error of at most 0.011.
Values may be sent and summed in bfloat16 or wider, within the bound.
A program may use at most 128 MiB of HBM per device.

v0:
```python
import math
import jax
import jax.numpy as jnp
from jax import lax
from jax.sharding import PartitionSpec as P


def sylvester(order_size):
    indices = jnp.arange(order_size, dtype=jnp.int32)
    common_bits = indices[:, None] & indices[None, :]
    parity = jnp.zeros((order_size, order_size), jnp.int32)
    for bit_number in range(order_size.bit_length()):
        parity = parity + (common_bits >> bit_number & 1)
    return (1 - 2 * (parity % 2)).astype(jnp.float32)


def spread(blocks, block_size):
    tok_rows = blocks.shape[0]
    local_blocks = blocks.shape[1] // block_size
    devices = lax.axis_size("tensor")
    norm_factor = 1.0 / math.sqrt(devices * local_blocks)
    hadamard = sylvester(devices * local_blocks).reshape(
        devices, local_blocks, devices, local_blocks
    )
    stacked = blocks.reshape(1, tok_rows, local_blocks, block_size)
    summed = jnp.einsum(
        "qtjc,qjpk->ptkc",
        lax.all_to_all(stacked, "tensor", split_axis=3, concat_axis=0, tiled=True).astype(
            jnp.float32
        ),
        hadamard,
        precision=lax.Precision.HIGHEST,
    )
    summed = (summed * norm_factor).astype(jnp.bfloat16)
    result = lax.all_to_all(summed, "tensor", split_axis=0, concat_axis=3, tiled=True)
    return result.reshape(tok_rows, local_blocks * block_size)


def on_device(out_grad, gate_act, up_act, codes, zero_points, scales, rotation):
    columns = gate_act.shape[1]
    block_size = rotation.shape[0]
    feat_rows = codes.shape[0]
    groups_here = scales.shape[1]
    group_cols = columns // groups_here
    gate32 = gate_act.astype(jnp.float32)
    up32 = up_act.astype(jnp.float32)
    sigmoid_gate = jax.nn.sigmoid(gate32)
    hidden = (gate32 * sigmoid_gate * up32).astype(jnp.bfloat16)
    mixed = jnp.dot(hidden, rotation, preferred_element_type=jnp.float32)
    mixed = mixed.astype(jnp.bfloat16)
    rotated = spread(mixed, block_size)
    levels = (codes.reshape(feat_rows, groups_here, group_cols) - zero_points[:, :, None]).astype(
        jnp.float32
    )
    weight = (levels * scales[:, :, None]).astype(jnp.bfloat16).reshape(feat_rows, columns)
    grad_slice = lax.all_to_all(out_grad, "dp", split_axis=1, concat_axis=0, tiled=True)
    weight_grad = lax.dot_general(
        grad_slice,
        lax.all_gather(rotated, "dp", axis=0, tiled=True),
        (((0,), (0,)), ((), ())),
        preferred_element_type=jnp.float32,
    )
    log_scale_grad = (
        jnp.sum(weight_grad.reshape(feat_rows, groups_here, group_cols) * levels, axis=2) * scales
    )
    grad_rotated = lax.psum_scatter(
        jnp.dot(grad_slice, weight, preferred_element_type=jnp.float32),
        "dp",
        scatter_dimension=0,
        tiled=True,
    )
    grad_mixed = spread(grad_rotated.astype(jnp.bfloat16), block_size)
    grad_hidden = lax.dot_general(
        grad_mixed, rotation, (((1,), (1,)), ((), ())), preferred_element_type=jnp.float32
    )
    grad_gate = (grad_hidden * up32 * sigmoid_gate * (1.0 + gate32 * (1.0 - sigmoid_gate))).astype(
        jnp.bfloat16
    )
    grad_up = (grad_hidden * gate32 * sigmoid_gate).astype(jnp.bfloat16)
    return (grad_gate, grad_up, log_scale_grad)


def solution(mesh):
    return jax.shard_map(
        on_device,
        mesh=mesh,
        in_specs=(
            P("dp", None),
            P("dp", "tensor"),
            P("dp", "tensor"),
            P("dp", "tensor"),
            P("dp", "tensor"),
            P("dp", "tensor"),
            P(),
        ),
        out_specs=(P("dp", "tensor"), P("dp", "tensor"), P("dp", "tensor")),
        check_vma=False,
    )
```

profile of v0, /device:TPU:90, one launch (start us, length us, event | category | flops | bytes accessed | tf_op | source)
XLA Modules:
  0.0 396.5 jit_solution(10725968039748546528)
XLA Ops:
  7.2 2.4 copy.24
  9.6 8.0 %all-to-all-start = ((bf16[128,16,320]{0,2,1:T(8,128)(2,1)}), bf16[128,16,320]{0,2,1:T(8,128)(2,1)}, u32[]{:S(2)}, u32[]{:S(2)}) async-start(bf16[128,16,320]{0,2,1:T(8,128)(2,1)} %bitcast.4), calls=%async_computation | async-start | bytes 2621440 | tf_op jit(solution)/shard_map/all_to_all | solution.py:56
  17.6 0.0 copy-start.1
  17.6 0.0 reduce-scatter.2.cloned.1.call-start
  17.7 2.4 copy.23
  20.0 0.0 copy-done
  20.1 0.0 copy-done.1
  20.1 1.3 fusion
  21.4 26.8 %all-to-all-done = bf16[128,16,320]{0,2,1:T(8,128)(2,1)} async-done(((bf16[128,16,320]{0,2,1:T(8,128)(2,1)}), bf16[128,16,320]{0,2,1:T(8,128)(2,1)}, u32[]{:S(2)}, u32[]{:S(2)}) %all-to-all-start) | async-done | bytes 1310752 | tf_op jit(solution)/shard_map/all_to_all | solution.py:56
  48.2 9.9 %convolution_bitcast_fusion = f32[2048,1600]{0,1:T(8,128)} fusion(bf16[320,1600]{0,1:T(8,128)(2,1)} %fusion, bf16[128,16,320]{0,2,1:T(8,128)(2,1)} %all-to-all-done), kind=kOutput, calls=%fused_computation | convolution fusion | flops 2097152000 | bytes 15441920 | tf_op jit(solution)/shard_map/dot_general | solution.py:67
  58.1 0.0 reduce-scatter.2.cloned.1.call-update
  58.1 0.5 all-gather.2.cloned.1.call-start
  58.6 0.5 copy-done.2
  59.1 0.1 copy-done.3
  59.2 4.7 %fusion.2 = bf16[1,128,1,1600]{1,3,2,0:T(8,128)(2,1)S(1)} fusion(bf16[1600,1600]{1,0:T(8,128)(2,1)} %param.13, bf16[128,1600]{0,1:T(8,128)(2,1)S(1)} %copy-done.3, bf16[128,1600]{0,1:T(8,128)(2,1)S(1)} %copy-done.2), kind=kOutput, calls=%fused_computation.8 | convolution fusion | flops 657203200 | bytes 6348800 | tf_op jit(solution)/shard_map/dot_general | solution.py:49
  63.9 6.4 %copy.55 = bf16[1,128,1,1600]{1,2,0,3:T(2,128)(2,1)S(1)} copy(bf16[1,128,1,1600]{1,3,2,0:T(8,128)(2,1)S(1)} %fusion.2) | data formatting | bytes 819200 | tf_op jit(solution)/shard_map/reshape | solution.py:25
  70.3 0.5 broadcast.409
  70.8 9.9 %reduce.5 = bf16[1600,128]{1,0:T(8,128)(2,1)} reduce(bf16[1600,1,1,128]{3,2,1,0:T(2,128)(2,1)S(1)} %bitcast.84, bf16[]{:T(256)} %broadcast.409), dimensions={1,2}, to_apply=%bitcast.80.reduce_sub_computation | reduce | bytes 819202
  80.7 1.1 reshape.191
  81.8 21.4 %all_to_all.79 = bf16[16,2,6400]{2,1,0:T(2,128)(2,1)} all-to-all(bf16[16,2,6400]{2,1,0:T(2,128)(2,1)S(1)} %reshape.191), channel_id=1, replica_groups=mesh['dp'=16,'tensor'=16] {'tensor'}, dimensions={0} | all-to-all | bytes 819200 | tf_op jit(solution)/shard_map/all_to_all | solution.py:28
  103.2 2.7 reshape.192
  106.0 7.6 %bitcast_reduce_fusion = bf16[128,1600]{0,1:T(8,128)(2,1)} fusion(bf16[1600,1,1,128]{3,2,1,0:T(2,128)(2,1)S(1)} %reshape.192), kind=kLoop, calls=%fused_computation.60 | loop fusion | bytes 819200 | tf_op jit(solution)/shard_map/all_to_all | solution.py:28
  113.6 1.1 all_to_all.69
  114.6 0.5 fusion.7
  115.1 0.1 copy.31
  115.3 18.8 %all_to_all.80 = bf16[16,128,1,100]{1,3,2,0:T(8,128)(2,1)S(1)} all-to-all(bf16[16,128,1,100]{1,3,2,0:T(8,128)(2,1)S(1)} %copy.31), channel_id=1, replica_groups=mesh['dp'=16,'tensor'=16] {'tensor'}, dimensions={0} | all-to-all | bytes 819200 | tf_op jit(solution)/shard_map/all_to_all | solution.py:35
  134.1 0.8 reshape.183
  134.9 0.0 all-gather.2.cloned.1.call-update
  134.9 83.6 %reduce-scatter.2.cloned.1.call-done = f32[128,1600]{0,1:T(8,128)} async-done(((f32[2048,1600]{0,1:T(8,128)}), f32[128,1600]{0,1:T(8,128)}) %reduce-scatter.2.cloned.1.call-update) | async-done | bytes 819216 | tf_op jit(solution)/shard_map/reduce_scatter | solution.py:66
  218.6 1.2 convert_bitcast_fusion
  219.8 6.4 %copy.56 = bf16[1,128,1,1600]{1,2,0,3:T(2,128)(2,1)S(1)} copy(bf16[1,128,1,1600]{1,3,2,0:T(8,128)(2,1)S(1)} %convert_bitcast_fusion) | data formatting | bytes 819200 | tf_op jit(solution)/shard_map/reshape | solution.py:25
  226.1 9.9 %reduce.4 = bf16[1600,128]{1,0:T(8,128)(2,1)} reduce(bf16[1600,1,1,128]{3,2,1,0:T(2,128)(2,1)S(1)} %bitcast.85, bf16[]{:T(256)} %broadcast.409), dimensions={1,2}, to_apply=%bitcast.81.reduce_sub_computation | reduce | bytes 819202
  236.0 1.1 reshape.189
  237.1 20.5 %all_to_all.81 = bf16[16,2,6400]{2,1,0:T(2,128)(2,1)} all-to-all(bf16[16,2,6400]{2,1,0:T(2,128)(2,1)S(1)} %reshape.189), channel_id=1, replica_groups=mesh['dp'=16,'tensor'=16] {'tensor'}, dimensions={0} | all-to-all | bytes 819200 | tf_op jit(solution)/shard_map/all_to_all | solution.py:28
  257.7 2.7 reshape.190
  260.4 7.6 %bitcast_reduce_fusion.1 = bf16[128,1600]{0,1:T(8,128)(2,1)} fusion(bf16[1600,1,1,128]{3,2,1,0:T(2,128)(2,1)S(1)} %reshape.190), kind=kLoop, calls=%fused_computation.61 | loop fusion | bytes 819200 | tf_op jit(solution)/shard_map/all_to_all | solution.py:28
  268.0 1.1 all_to_all.63
  269.1 0.5 fusion.8
  269.6 0.9 copy.28
  270.5 5.8 %all-to-all-start.2 = ((bf16[16,128,1,100]{1,3,2,0:T(8,128)(2,1)}), bf16[16,128,1,100]{1,3,2,0:T(8,128)(2,1)S(1)}, u32[]{:S(2)}, u32[]{:S(2)}) async-start(bf16[16,128,1,100]{1,3,2,0:T(8,128)(2,1)} %copy.28), calls=%async_computation.3 | async-start | bytes 851968 | tf_op jit(solution)/shard_map/all_to_all | solution.py:35
  276.3 94.5 %all-gather.2.cloned.1.call-done = bf16[2048,1600]{0,1:T(8,128)(2,1)} async-done(((bf16[128,1600]{0,1:T(8,128)(2,1)}), bf16[2048,1600]{0,1:T(8,128)(2,1)}) %all-gather.2.cloned.1.call-update) | async-done | bytes 6553616 | tf_op jit(solution)/shard_map/all_gather | solution.py:59
  370.8 7.1 %convolution_bitcast_fusion.1 = f32[320,1600]{1,0:T(8,128)} fusion(bf16[2048,1600]{0,1:T(8,128)(2,1)} %all-gather.2.cloned.1.call-done, bf16[128,16,320]{0,2,1:T(8,128)(2,1)} %all-to-all-done), kind=kOutput, calls=%fused_computation.1 | convolution fusion | flops 2097152000 | bytes 9912320 | tf_op jit(solution)/shard_map/dot_general | solution.py:57
  377.9 3.1 copy.32
  381.0 2.3 multiply_reduce_fusion
  383.3 0.6 mul.90
  384.0 0.0 all-to-all-done.2
  384.0 0.1 reshape.180
  384.0 5.3 %fusion.20 = (bf16[128,1600]{0,1:T(8,128)(2,1)}, bf16[128,1600]{0,1:T(8,128)(2,1)}) fusion(bf16[128,1600]{0,1:T(8,128)(2,1)} %param.8, bf16[128,1600]{0,1:T(8,128)(2,1)} %param.9, bf16[1600,1600]{1,0:T(8,128)(2,1)} %param.13, bf16[128,1600]{0,1:T(8,128)(2,1)S(1)} %reshape.180), kind=kOutput, calls=%fused_computation.34 | convolution fusion | flops 658432000 | bytes 7168000 | tf_op jit(solution)/shard_map/dot_general | solution.py:73
  (3 shorter events, 0.0 us)
Async XLA Ops:
  9.6 38.6 %all-to-all-start = ((bf16[128,16,320]{0,2,1:T(8,128)(2,1)}), bf16[128,16,320]{0,2,1:T(8,128)(2,1)}, u32[]{:S(2)}, u32[]{:S(2)}) async-start(bf16[128,16,320]{0,2,1:T(8,128)(2,1)} %bitcast.4), calls=%async_computation | async-start | bytes 2621440 | tf_op jit(solution)/shard_map/all_to_all | solution.py:56
  17.6 2.4 copy-start
  17.6 2.4 copy-start.1
  17.6 200.9 %reduce-scatter.2.cloned.1.call-start = ((), (), s32[]{:S(2)}) async-start(), calls=%async_computation.6 | async-start | bytes 13926400 | tf_op jit(solution)/shard_map/reduce_scatter | solution.py:66
  58.1 1.0 copy-start.2
  58.1 1.1 copy-start.3
  58.1 312.7 %all-gather.2.cloned.1.call-start = ((), (), s32[]{:S(2)}) async-start(), calls=%async_computation.7 | async-start | bytes 6963200 | tf_op jit(solution)/shard_map/all_gather | solution.py:59
  270.5 113.5 %all-to-all-start.2 = ((bf16[16,128,1,100]{1,3,2,0:T(8,128)(2,1)}), bf16[16,128,1,100]{1,3,2,0:T(8,128)(2,1)S(1)}, u32[]{:S(2)}, u32[]{:S(2)}) async-start(bf16[16,128,1,100]{1,3,2,0:T(8,128)(2,1)} %copy.28), calls=%async_computation.3 | async-start | bytes 851968 | tf_op jit(solution)/shard_map/all_to_all | solution.py:35
Sparse Core Ops, SparseCore 0:
  58.3 160.2 reduce-scatter.1
  220.9 149.8 all-gather.1
where the time goes:
time: 401 us; the launch traced here: 396 us
  waiting for transfers between devices  205 us (51%)
  blocking collectives  60.8 us (15%)
  local copies, waits for them, and re-layouts  48.7 us (12%)
  matrix products  28 us (7%)
  other arithmetic  25.3 us (6%)
  starting transfers between devices  14.4 us (4%)
  between operations  14.4 us (4%)
    all_gather x1, waiting for transfers between devices, on_device(): lax.all_gather(rotated, 'dp', axis=0, tiled=True)  94.5 us
    reduce_scatter x1, waiting for transfers between devices, on_device(): lax.psum_scatter(jnp.dot(grad_slice, weight, preferred_element_type=jnp.f...  83.6 us
    all_to_all x2, blocking collectives, spread(): lax.all_to_all(stacked, 'tensor', split_axis=3, concat_axis=0, tiled=True)  41.9 us
    all_to_all x1, waiting for transfers between devices, on_device(): lax.all_to_all(out_grad, 'dp', split_axis=1, concat_axis=0, tiled=True)  26.8 us
    unnamed x2, other arithmetic  19.8 us
    all_to_all x1, blocking collectives, spread(): lax.all_to_all(summed, 'tensor', split_axis=0, concat_axis=3, tiled=True)  18.8 us
    all_to_all x4, local copies, waits for them, and re-layouts, spread(): lax.all_to_all(stacked, 'tensor', split_axis=3, concat_axis=0, tiled=True)  17.3 us
    unnamed x15, local copies, waits for them, and re-layouts  13.6 us
  transfers between devices with their start and end apart: 4, of which 3 were waited for; matrix products, arithmetic and copies ran while one was open for 21% of the time, Pallas kernels for 0%

commit v1 on v0

--- a/solution.py
+++ b/solution.py
@@ -1,8 +1,22 @@
+import functools
 import math
 import jax
 import jax.numpy as jnp
 from jax import lax
 from jax.sharding import PartitionSpec as P
+
+
+def raise_stages_all(m, along_dim, dim_k):
+    seen_now = jnp.concatenate(
+        jax.lax.all_to_all(
+            jnp.stack(jnp.split(m, jax.lax.axis_size("tensor"), along_dim), 0), "tensor", 0, 0
+        ),
+        dim_k,
+    )
+    return seen_now
+
+
+assign_words_for = functools.partial(raise_stages_all, along_dim=3, dim_k=0)
 
 
 def sylvester(order_size):
@@ -25,9 +39,7 @@
     stacked = blocks.reshape(1, tok_rows, local_blocks, block_size)
     summed = jnp.einsum(
         "qtjc,qjpk->ptkc",
-        lax.all_to_all(stacked, "tensor", split_axis=3, concat_axis=0, tiled=True).astype(
-            jnp.float32
-        ),
+        assign_words_for(stacked).astype(jnp.float32),
         hadamard,
         precision=lax.Precision.HIGHEST,
     )

time: 401 us -> 388 us (0.968)
  waiting for transfers between devices: 205 us -> 249 us
  local copies, waits for them, and re-layouts: 48.7 us -> 11.4 us
  other arithmetic: 25.3 us -> 5.46 us
    reduce_scatter x1, waiting for transfers between devices: 83.6 us -> 113 us  [on_device(): lax.psum_scatter(jnp.dot(grad_slice, weight, preferred_element_type=jnp.f...]
    unnamed x2 -> x0, other arithmetic: 19.8 us -> none
    all_to_all x4 -> x0, local copies, waits for them, and re-layouts: 17.3 us -> none  [spread(): lax.all_to_all(stacked, 'tensor', split_axis=3, concat_axis=0, tiled=True)]
    all_gather x1, waiting for transfers between devices: 94.5 us -> 110 us  [on_device(): lax.all_gather(rotated, 'dp', axis=0, tiled=True)]
    reshape x2 -> x0, local copies, waits for them, and re-layouts: 12.7 us -> none  [spread(): stacked = blocks.reshape(1, tok_rows, local_blocks, block_size)]
    unnamed x15 -> x40, local copies, waits for them, and re-layouts: 13.6 us -> 6.28 us
  transfers between devices with their start and end apart: 4 -> 4, of which waited for: 3 -> 3; matrix products, arithmetic and copies ran while one was open for 21% -> 7% of each run, Pallas kernels for 0% -> 0%
where the time goes in v1:
time: 388 us; the launch traced here: 383 us
  waiting for transfers between devices  249 us (64%)
  blocking collectives  60.6 us (16%)
  matrix products  27.9 us (7%)
  between operations  14.3 us (4%)
  starting transfers between devices  13.9 us (4%)
  local copies, waits for them, and re-layouts  11.4 us (3%)
  other arithmetic  5.46 us (1%)
    reduce_scatter x1, waiting for transfers between devices, on_device(): lax.psum_scatter(jnp.dot(grad_slice, weight, preferred_element_type=jnp.f...  113 us
    all_gather x1, waiting for transfers between devices, on_device(): lax.all_gather(rotated, 'dp', axis=0, tiled=True)  110 us
    all_to_all x2, blocking collectives, raise_stages_all(): jax.lax.all_to_all(jnp.stack(jnp.split(m, jax.lax.axis_size('tensor'), al...  41.8 us
    all_to_all x1, waiting for transfers between devices, on_device(): lax.all_to_all(out_grad, 'dp', split_axis=1, concat_axis=0, tiled=True)  26.8 us
    all_to_all x1, blocking collectives, spread(): lax.all_to_all(summed, 'tensor', split_axis=0, concat_axis=3, tiled=True)  18.8 us
    dot_general x1, matrix products, on_device(): jnp.dot(grad_slice, weight, preferred_element_type=jnp.float32)  9.93 us
    all_to_all x1, starting transfers between devices, on_device(): lax.all_to_all(out_grad, 'dp', split_axis=1, concat_axis=0, tiled=True)  8 us
  transfers between devices with their start and end apart: 4, of which 3 were waited for; matrix products, arithmetic and copies ran while one was open for 7% of the time, Pallas kernels for 0%

profile of v1, /device:TPU:90, one launch (start us, length us, event | category | flops | bytes accessed | tf_op | source)
XLA Modules:
  0.0 382.9 jit_solution(16542730054971142537)
XLA Ops:
  7.2 2.4 copy.24
  9.6 8.0 %all-to-all-start = ((bf16[128,16,320]{0,2,1:T(8,128)(2,1)}), bf16[128,16,320]{0,2,1:T(8,128)(2,1)}, u32[]{:S(2)}, u32[]{:S(2)}) async-start(bf16[128,16,320]{0,2,1:T(8,128)(2,1)} %bitcast.4), calls=%async_computation | async-start | bytes 2621440 | tf_op jit(solution)/shard_map/all_to_all | solution.py:68
  17.6 0.0 copy-start
  17.6 0.0 copy-start.1
  17.6 0.0 reduce-scatter.2.cloned.1.call-start
  17.7 2.4 copy.23
  20.0 0.0 copy-done
  20.1 0.0 copy-done.1
  20.1 1.3 fusion
  21.4 26.8 %all-to-all-done = bf16[128,16,320]{0,2,1:T(8,128)(2,1)} async-done(((bf16[128,16,320]{0,2,1:T(8,128)(2,1)}), bf16[128,16,320]{0,2,1:T(8,128)(2,1)}, u32[]{:S(2)}, u32[]{:S(2)}) %all-to-all-start) | async-done | bytes 1310752 | tf_op jit(solution)/shard_map/all_to_all | solution.py:68
  48.2 9.9 %convolution_bitcast_fusion = f32[2048,1600]{0,1:T(8,128)} fusion(bf16[320,1600]{0,1:T(8,128)(2,1)} %fusion, bf16[128,16,320]{0,2,1:T(8,128)(2,1)} %all-to-all-done), kind=kOutput, calls=%fused_computation | convolution fusion | flops 2097152000 | bytes 15441920 | tf_op jit(solution)/shard_map/dot_general | solution.py:79
  58.1 0.0 copy-start.2
  58.1 0.0 copy-start.3
  58.1 0.0 reduce-scatter.2.cloned.1.call-update
  58.1 0.0 all-gather.2.cloned.1.call-start
  58.2 0.9 copy-done.2
  59.1 0.1 copy-done.3
  59.2 4.7 %fusion.2 = bf16[1,128,1,1600]{1,3,2,0:T(8,128)(2,1)S(1)} fusion(bf16[1600,1600]{1,0:T(8,128)(2,1)} %param.13, bf16[128,1600]{0,1:T(8,128)(2,1)S(1)} %copy-done.3, bf16[128,1600]{0,1:T(8,128)(2,1)S(1)} %copy-done.2), kind=kOutput, calls=%fused_computation.8 | convolution fusion | flops 657203200 | bytes 6348800 | tf_op jit(solution)/shard_map/dot_general | solution.py:61
  64.3 21.5 %all_to_all.59 = bf16[16,1,128,1,100]{2,4,3,1,0:T(8,128)(2,1)S(1)} all-to-all(bf16[16,1,128,1,100]{2,4,3,1,0:T(8,128)(2,1)S(1)} %constant_dynamic-update-slice_fusion.16), channel_id=1, replica_groups=mesh['dp'=16,'tensor'=16] {'tensor'}, dimensions={0} | all-to-all | bytes 819200 | tf_op jit(solution)/shard_map/all_to_all | solution.py:11
  85.7 0.5 fusion.7
  86.2 0.1 copy.29
  86.3 18.8 %all_to_all.60 = bf16[16,128,1,100]{1,3,2,0:T(8,128)(2,1)S(1)} all-to-all(bf16[16,128,1,100]{1,3,2,0:T(8,128)(2,1)S(1)} %copy.29), channel_id=1, replica_groups=mesh['dp'=16,'tensor'=16] {'tensor'}, dimensions={0} | all-to-all | bytes 819200 | tf_op jit(solution)/shard_map/all_to_all | solution.py:47
  105.1 0.8 reshape.185
  106.0 0.0 all-gather.2.cloned.1.call-update
  106.0 112.9 %reduce-scatter.2.cloned.1.call-done = f32[128,1600]{0,1:T(8,128)} async-done(((f32[2048,1600]{0,1:T(8,128)}), f32[128,1600]{0,1:T(8,128)}) %reduce-scatter.2.cloned.1.call-update) | async-done | bytes 819216 | tf_op jit(solution)/shard_map/reduce_scatter | solution.py:78
  218.9 1.2 convert_bitcast_fusion
  220.4 20.3 %all_to_all.61 = bf16[16,1,128,1,100]{2,4,3,1,0:T(8,128)(2,1)S(1)} all-to-all(bf16[16,1,128,1,100]{2,4,3,1,0:T(8,128)(2,1)S(1)} %constant_dynamic-update-slice_fusion), channel_id=1, replica_groups=mesh['dp'=16,'tensor'=16] {'tensor'}, dimensions={0} | all-to-all | bytes 819200 | tf_op jit(solution)/shard_map/all_to_all | solution.py:11
  240.7 0.5 fusion.8
  241.2 0.9 copy.27
  242.0 5.8 %all-to-all-start.2 = ((bf16[16,128,1,100]{1,3,2,0:T(8,128)(2,1)}), bf16[16,128,1,100]{1,3,2,0:T(8,128)(2,1)S(1)}, u32[]{:S(2)}, u32[]{:S(2)}) async-start(bf16[16,128,1,100]{1,3,2,0:T(8,128)(2,1)} %copy.27), calls=%async_computation.3 | async-start | bytes 851968 | tf_op jit(solution)/shard_map/all_to_all | solution.py:47
  247.8 109.7 %all-gather.2.cloned.1.call-done = bf16[2048,1600]{0,1:T(8,128)(2,1)} async-done(((bf16[128,1600]{0,1:T(8,128)(2,1)}), bf16[2048,1600]{0,1:T(8,128)(2,1)}) %all-gather.2.cloned.1.call-update) | async-done | bytes 6553616 | tf_op jit(solution)/shard_map/all_gather | solution.py:71
  357.5 7.1 %convolution_bitcast_fusion.1 = f32[320,1600]{1,0:T(8,128)} fusion(bf16[2048,1600]{0,1:T(8,128)(2,1)} %all-gather.2.cloned.1.call-done, bf16[128,16,320]{0,2,1:T(8,128)(2,1)} %all-to-all-done), kind=kOutput, calls=%fused_computation.1 | convolution fusion | flops 2097152000 | bytes 9912320 | tf_op jit(solution)/shard_map/dot_general | solution.py:69
  364.6 3.2 copy.30
  367.7 2.3 multiply_reduce_fusion
  370.1 0.6 mul.90
  370.7 0.0 all-to-all-done.2
  370.7 0.1 reshape.182
  370.8 5.2 %fusion.20 = (bf16[128,1600]{0,1:T(8,128)(2,1)}, bf16[128,1600]{0,1:T(8,128)(2,1)}) fusion(bf16[128,1600]{0,1:T(8,128)(2,1)S(1)} %copy-done.2, bf16[128,1600]{0,1:T(8,128)(2,1)} %param.9, bf16[1600,1600]{1,0:T(8,128)(2,1)} %param.13, bf16[128,1600]{0,1:T(8,128)(2,1)S(1)} %reshape.182), kind=kOutput, calls=%fused_computation.34 | convolution fusion | flops 658432000 | bytes 7168000 | tf_op jit(solution)/shard_map/dot_general | solution.py:85
  (32 shorter events, 0.5 us)
Async XLA Ops:
  9.6 38.6 %all-to-all-start = ((bf16[128,16,320]{0,2,1:T(8,128)(2,1)}), bf16[128,16,320]{0,2,1:T(8,128)(2,1)}, u32[]{:S(2)}, u32[]{:S(2)}) async-start(bf16[128,16,320]{0,2,1:T(8,128)(2,1)} %bitcast.4), calls=%async_computation | async-start | bytes 2621440 | tf_op jit(solution)/shard_map/all_to_all | solution.py:68
  17.6 2.4 copy-start
  17.6 2.4 copy-start.1
  17.6 201.2 %reduce-scatter.2.cloned.1.call-start = ((), (), s32[]{:S(2)}) async-start(), calls=%async_computation.6 | async-start | bytes 13926400 | tf_op jit(solution)/shard_map/reduce_scatter | solution.py:78
  58.1 1.0 copy-start.2
  58.1 1.1 copy-start.3
  58.1 299.4 %all-gather.2.cloned.1.call-start = ((), (), s32[]{:S(2)}) async-start(), calls=%async_computation.7 | async-start | bytes 6963200 | tf_op jit(solution)/shard_map/all_gather | solution.py:71
  242.0 128.7 %all-to-all-start.2 = ((bf16[16,128,1,100]{1,3,2,0:T(8,128)(2,1)}), bf16[16,128,1,100]{1,3,2,0:T(8,128)(2,1)S(1)}, u32[]{:S(2)}, u32[]{:S(2)}) async-start(bf16[16,128,1,100]{1,3,2,0:T(8,128)(2,1)} %copy.27), calls=%async_computation.3 | async-start | bytes 851968 | tf_op jit(solution)/shard_map/all_to_all | solution.py:47
Sparse Core Ops, SparseCore 0:
  58.3 160.5 reduce-scatter.1
  221.1 136.3 all-gather.1
